TPU v7x, 32 devices: a whole 2x2x4 slice. The times are simulated.
32 devices in a mesh: gx: 4 (over z), gy: 8 (over y, x, core).
Axes of the slice: x: 2, y: 2, z: 4, core: 2. Of those that a mesh axis runs over, the one named last changes fastest.
Arguments:
- positions: float32 [3, 4, 8, 2048], P(None, 'gx', 'gy'), as said below
- velocities: float32 [3, 4, 8, 2048], P(None, 'gx', 'gy'), may hold values from -0.1 to 0.1
- bead_types: int32 [4, 8, 2048], P('gx', 'gy'), may hold values from 0 to 18, as said below
- eps_table: float32 [18, 18], replicated, may hold values from 2 to 5.6
- charges: float32 [18], replicated, may hold values from -1 to 1
- x_list: int32 [4, 8, 512], P('gx', 'gy'), may hold values from 0 to 2047, as said below
- y_list: int32 [4, 8, 512], P('gx', 'gy'), may hold values from 0 to 2047, as said below
- tiles: int32 [4, 8, 2, 112], P('gx', 'gy'), may hold values from 0 to 26, as said below
Outputs:
- new_positions: float32 [3, 4, 8, 2048], P(None, 'gx', 'gy')
- new_velocities: float32 [3, 4, 8, 2048], P(None, 'gx', 'gy')
Inputs may be any that keep to these rules, and one draw needn't show every extreme that they name: `positions`: each column's slots fill a lattice of 8 x 8 x 32 sites of spacing 0.43 nm in the column's frame, one slot a site; slots 128 * c to 128 * c + 127 hold the sites of layers 2c and 2c + 1 in some order, and each bead lies within 0.03 nm of its site in every coordinate. `bead_types`: type 18 marks an empty slot; a column's empty slots are exactly its sites in layers at or above its filled height, a multiple of 2 from 2 to 32; columns (0 or 1, 0 or 1) are full. `x_list`: entry e names the slot at the site with x index e % 2, y index (e // 2) % 8 and layer e // 16. `y_list`: entry e names the slot at the site with x index e % 8, y index (e // 8) % 2 and layer e // 16. Zone clusters 0 to 24 are the own, x-import, y-import and corner clusters in the order of the zone beads; a column's real tiles come first, at most 101 of them, reached by column (0, 0), and every later slot holds the pair (25, 26).
All inputs are finite; a program needn't handle non-finite values.
Results may differ from a plain program's by a relative error of at most 0.0003.
Values sent between devices are 32-bit elements; how exact they have to be, the bound alone decides.
A program may use at most 64 MiB of HBM per device.

v0:
```python
import functools

import jax
import jax.numpy as jnp
from jax import lax
from jax.experimental import pallas as pl
from jax.experimental.pallas import tpu as pltpu
from jax.sharding import PartitionSpec as P

NTYPES = 18
STEPS = 4
SPACING = 0.43
CUTOFF = 1.1
SIGMA = 0.41
COULOMB = 138.935458 / 15.0
MASS = 72.0
TIME_STEP = 0.02

MESH = pl.DeviceIdType.MESH
ROWS = 16
LANES = 128
HALO = 8
NONE = 31
SIDES = [(-1, -1), (-1, 0), (-1, 1), (0, -1), (0, 1), (1, -1), (1, 0), (1, 1)]
ZONES = [(0, 0), (1, 0), (0, 1), (1, 1)]
NEAR = [(dx, dy) for dy in range(-2, 3) for dx in range(-2, 3) if 0 < dx * dx + dy * dy <= 4]
MIDDLE = [(dx, dy) for dy in range(-2, 3) for dx in range(-2, 3) if dx * dx + dy * dy == 5]
FAR = [(dx, dy) for dy in range(-2, 3) for dx in range(-2, 3) if dx * dx + dy * dy == 8]
SHIFTS = NEAR + MIDDLE + FAR + [(0, 0)]
RUNS = [
    (0, len(NEAR), (-2, -1, 0, 1, 2), 0),
    (len(NEAR), len(MIDDLE), (-1, 0, 1), 5 * len(NEAR)),
    (len(NEAR) + len(MIDDLE), len(FAR), (0,), 5 * len(NEAR) + 3 * len(MIDDLE)),
    (len(SHIFTS) - 1, 1, (-2, -1, 1, 2), 5 * len(NEAR) + 3 * len(MIDDLE) + len(FAR)),
]
COUNT = RUNS[3][3] + 4
UNIT = SIGMA * 2.0 ** (1.0 / 6.0)
REACH = (CUTOFF / UNIT) ** 2
TAPER = (UNIT / CUTOFF) ** 4
LJ_FACTOR = 12.0 / UNIT**2 * TAPER
Q_FACTOR = COULOMB / UNIT**3 * TAPER
Q_SHIFT = (UNIT / CUTOFF) ** 3
AHEAD = 3


def lane_gather(values, index):
    return jnp.take_along_axis(values, index, axis=1)


def kernel(
    n_gx, n_gy, side,
    pos_ref, vel_ref, kind_ref, tile_ref, eps_ref, charge_ref,
    out_pos_ref, out_vel_ref,
    tile_send, tile_recv, send, recv, ext, kind_ext, charge_ext, coef_lj, coef_q, now, speed, mix, site_ref, square, eps_own,
    tile_sems, send_sems, recv_sems,
):
    width = side * SPACING
    my_x = lax.axis_index("gx")
    my_y = lax.axis_index("gy")

    def at(sx, sy):
        return (
            lax.rem(my_x + (sx + n_gx), n_gx),
            lax.rem(my_y + (sy + n_gy), n_gy),
        )

    barrier = pltpu.get_barrier_semaphore()
    for sx, sy in SIDES:
        pl.semaphore_signal(barrier, inc=1, device_id=at(sx, sy), device_id_type=MESH)

    lane = lax.broadcasted_iota(jnp.int32, (ROWS, LANES), 1)
    row = lax.broadcasted_iota(jnp.int32, (ROWS, LANES), 0)
    lane8 = lane[:8]
    half = lane >> 6
    y_site = (lane >> 3) & 7
    x_site = lane & 7
    low_half = lane8 < 64

    tile_send[...] = jnp.full((8, LANES), NONE - 1, jnp.int32)
    tile_send[0:2, 0 : tile_ref.shape[1]] = tile_ref[...]

    cluster = row
    sx_f = jnp.floor(pos_ref[0] * (1.0 / SPACING) + 0.5)
    sy_f = jnp.floor(pos_ref[1] * (1.0 / SPACING) + 0.5)
    sz_f = jnp.floor(pos_ref[2] * (1.0 / SPACING) + 0.5)
    site = (
        (sz_f.astype(jnp.int32) - 2 * cluster) * 64
        + sy_f.astype(jnp.int32) * 8
        + sx_f.astype(jnp.int32)
    )
    site = jnp.clip(site, 0, LANES - 1)
    site_ref[...] = site
    big_row = lax.broadcasted_iota(jnp.int32, (LANES, LANES), 0)
    row8 = row[:8]
    parts = []
    for part in range(2):
        total = jnp.zeros((8, LANES), jnp.float32)
        for sub in range(8):
            here = site[part * 8 + sub : part * 8 + sub + 1, :]
            onehot = jnp.where(big_row == here, 1.0, 0.0).astype(jnp.bfloat16)
            left = jnp.where(row8 == sub, lane8, 0).astype(jnp.float32).astype(jnp.bfloat16)
            total = total + lax.dot_general(
                left, onehot, (((1,), (1,)), ((), ())), preferred_element_type=jnp.float32
            )
        parts.append(total)
    slot = jnp.concatenate(parts, axis=0).astype(jnp.int32)

    def to_lattice(values):
        ordered = lane_gather(values, slot)
        first, second = ordered[:8], ordered[8:]
        even = jnp.where(low_half, first, pltpu.roll(second, 64, 1))
        odd = jnp.where(low_half, pltpu.roll(first, 64, 1), second)
        mix[pl.ds(0, 8, stride=2), :] = even
        mix[pl.ds(1, 8, stride=2), :] = odd
        return mix[...]

    def to_slots(values):
        mix[...] = values
        even = mix[pl.ds(0, 8, stride=2), :]
        odd = mix[pl.ds(1, 8, stride=2), :]
        first = jnp.where(low_half, even, pltpu.roll(odd, 64, 1))
        second = jnp.where(low_half, pltpu.roll(even, 64, 1), odd)
        return lane_gather(jnp.concatenate([first, second], axis=0), site_ref[...])

    for component in range(3):
        now[component] = to_lattice(pos_ref[component])
        speed[component] = to_lattice(vel_ref[component])
    kind = to_lattice(kind_ref[...].astype(jnp.float32))

    def pack_index(sx, sy):
        if sx != 0 and sy != 0:
            slot_of = lane >> 3
            inner = lane & 7
            zh, yb, xb = inner >> 2, (inner >> 1) & 1, inner & 1
        elif sx != 0:
            slot_of = lane >> 5
            inner = lane & 31
            zh, yb, xb = inner >> 4, (inner >> 1) & 7, inner & 1
        else:
            slot_of = lane >> 5
            inner = lane & 31
            zh, yb, xb = inner >> 4, (inner >> 3) & 1, inner & 7
        x_low = side - 2 if sx > 0 else 0
        y_low = side - 2 if sy > 0 else 0
        return slot_of, zh * 64 + (yb + y_low) * 8 + xb + x_low

    def unpack_index(sx, sy):
        if sx != 0 and sy != 0:
            return half * 4 + (y_site & 1) * 2 + (x_site & 1), 8
        if sx != 0:
            return half * 16 + y_site * 2 + (x_site & 1), 32
        return half * 16 + (y_site & 1) * 8 + x_site, 32

    def pack(values, sx, sy):
        slot_of, source = pack_index(sx, sy)
        packed = lane_gather(values[0], source)
        for component in range(1, len(values)):
            packed = jnp.where(slot_of == component, lane_gather(values[component], source), packed)
        return packed

    def side_copy(turn, number):
        sx, sy = SIDES[number]
        return pltpu.make_async_remote_copy(
            src_ref=send.at[turn, number],
            dst_ref=recv.at[turn, number],
            send_sem=send_sems.at[turn, number],
            recv_sem=recv_sems.at[turn, number],
            device_id=at(sx, sy),
            device_id_type=MESH,
        )

    def tile_copy(number):
        sx, sy = ZONES[number + 1]
        return pltpu.make_async_remote_copy(
            src_ref=tile_send,
            dst_ref=tile_recv.at[number],
            send_sem=tile_sems.at[0, number],
            recv_sem=tile_sems.at[1, number],
            device_id=at(sx, sy),
            device_id_type=MESH,
        )

    def image(turn, ux, uy, component):
        number = SIDES.index((-ux, -uy))
        index, stride = unpack_index(ux, uy)
        return lane_gather(recv[turn, number], index + component * stride)

    def merge_and_shift(images, dx, dy):
        merged = images[(0, 0)]
        in_x = (x_site < dx) if dx > 0 else (x_site >= side + dx)
        in_y = (y_site < dy) if dy > 0 else (y_site >= side + dy)
        ux = (dx > 0) - (dx < 0)
        uy = (dy > 0) - (dy < 0)
        if dx != 0:
            merged = jnp.where(in_x, images[(ux, 0)], merged)
        if dy != 0:
            outer = images[(0, uy)]
            if dx != 0:
                outer = jnp.where(in_x, images[(ux, uy)], outer)
            merged = jnp.where(in_y, outer, merged)
        if dx == 0 and dy == 0:
            return merged
        source = half * 64 + ((y_site + dy) & 7) * 8 + ((x_site + dx) & 7)
        return lane_gather(merged, source)

    def put_extended(ref, values):
        ref[pl.ds(HALO, ROWS), :] = values
        turned = pltpu.roll(jnp.where(row8 < 4, values[:8], values[8:]), 64, 1)
        ref[pl.ds(0, HALO), :] = turned
        ref[pl.ds(HALO + ROWS, HALO), :] = turned

    def gather_images(turn, component, own):
        images = {(0, 0): own}
        for ux, uy in SIDES:
            got = image(turn, ux, uy, component)
            if component == 0 and ux != 0:
                got = got + ux * width
            if component == 1 and uy != 0:
                got = got + uy * width
            images[(ux, uy)] = got
        return images

    def exchange(turn, values):
        for number, (sx, sy) in enumerate(SIDES):
            send[turn, number] = pack(values, sx, sy)
        for number in range(len(SIDES)):
            side_copy(turn, number).start()

    def spread_position(images, number):
        dx, dy = SHIFTS[number]
        for component in range(3):
            put_extended(ext.at[number, component], merge_and_shift(images[component], dx, dy))

    square[...] = jnp.zeros((LANES, LANES), jnp.float32)
    square[0:NTYPES, 0:NTYPES] = eps_ref[...]
    padded = square[...]
    square[...] = (padded + padded.T) * (0.5 * LJ_FACTOR)
    mix[0:1, :] = jnp.zeros((1, LANES), jnp.float32)
    mix[0:1, 0:NTYPES] = charge_ref[...]
    charge_row = jnp.broadcast_to(mix[0:1, :], (ROWS, LANES))

    pl.semaphore_wait(barrier, len(SIDES))
    own = [now[component] for component in range(3)]
    exchange(0, own + [kind])
    for number in range(3):
        tile_copy(number).start()
    for number in range(len(SIDES)):
        side_copy(0, number).wait_recv()
    for number in range(3):
        tile_copy(number).wait_recv()

    iota_small = lax.broadcasted_iota(jnp.int32, (32, LANES), 0)
    lane_small = lax.broadcasted_iota(jnp.int32, (32, LANES), 1)
    count_row = lax.broadcasted_iota(jnp.int32, (ROWS, 32), 0)
    count_lane = lax.broadcasted_iota(jnp.int32, (ROWS, 32), 1)
    nt = (((1,), (1,)), ((), ()))

    def onehot_of(condition):
        return jnp.where(condition, 1.0, 0.0).astype(jnp.bfloat16)

    tables = []
    for pair in range(2):
        table = jnp.zeros((ROWS, LANES), jnp.float32)
        for zone in (2 * pair, 2 * pair + 1):
            source = tile_send if zone == 0 else tile_recv.at[zone - 1]
            first = source[0:1, :]
            second = source[1:2, :]
            base = 32 * (zone & 1)
            small_a = onehot_of(iota_small == first)
            small_b = onehot_of(iota_small == second)
            place = big_row - base
            big_a = onehot_of((place == first) | (place == first + 64))
            big_b = onehot_of((place == second) | (place == second + 64))
            forth = lax.dot_general(small_a, big_b, nt, preferred_element_type=jnp.float32)
            back = lax.dot_general(small_b, big_a, nt, preferred_element_type=jnp.float32)
            on_diagonal = (lane_small & 63) == iota_small + base
            counts = jnp.where(on_diagonal, forth, forth + back).astype(jnp.bfloat16)
            picked = []
            for zh in range(2):
                layer = zh * ROWS + count_row
                if zone == 0:
                    which = layer >> 1
                elif zone == 1:
                    which = 16 + (layer >> 3)
                elif zone == 2:
                    which = 20 + (layer >> 3)
                else:
                    which = jnp.full_like(layer, 24)
                picked.append(
                    jnp.dot(onehot_of(count_lane == which), counts, preferred_element_type=jnp.float32)
                )
            table = table + jnp.where(half == 0, picked[0], picked[1])
        tables.append(table)

    cat_x, cat_y = (lane >> 2) & 3, lane & 3
    weight_of = {}
    for dz in range(-2, 3):
        layer = half * ROWS + row + dz
        in_z = (layer >= 0) & (layer < 2 * ROWS)
        total = jnp.zeros((ROWS, LANES), jnp.float32)
        for zone, (ox, oy) in enumerate(ZONES):
            on_x = (cat_x >= 2) if ox else (cat_x <= 2)
            on_y = (cat_y >= 2) if oy else (cat_y <= 2)
            in_x = cat_x == (2 if ox else 1)
            in_y = cat_y == (2 if oy else 1)
            start = jnp.where(in_x, jnp.where(in_y, 24, 16), jnp.where(in_y, 20, 0))
            shift = jnp.where(in_x, jnp.where(in_y, 6, 3), jnp.where(in_y, 3, 1))
            which = jnp.where(on_x & on_y & in_z, start + (layer >> shift), NONE)
            total = total + lane_gather(tables[zone >> 1], half * 64 + 32 * (zone & 1) + which)
        weight_of[dz] = total

    def category(site, step):
        other = site + step
        return jnp.where(
            other >= side, 1, jnp.where(other < 0, 3, jnp.where((site < 2) & (other < 2), 2, 0))
        )

    kind_images = gather_images(0, 3, kind)
    kind_images = {key: value.astype(jnp.int32) for key, value in kind_images.items()}
    charge_images = {key: lane_gather(charge_row, value) for key, value in kind_images.items()}
    kind_own = kind_images[(0, 0)]
    for k in range(NTYPES):
        row_k = jnp.broadcast_to(square[k : k + 1, :], (ROWS, LANES))
        eps_own[k] = lane_gather(row_k, kind_own)

    def depth_of(other):
        level = [eps_own[k] for k in range(NTYPES)] + [jnp.zeros((ROWS, LANES), jnp.float32)]
        bit = 1
        while len(level) > 1:
            odd = (other & bit) != 0
            joined = [jnp.where(odd, level[k + 1], level[k]) for k in range(0, len(level) - 1, 2)]
            if len(level) % 2:
                joined.append(level[-1])
            level = joined
            bit = 2 * bit
        return level[0]

    def spread_kind(number):
        dx, dy = SHIFTS[number]
        put_extended(kind_ext.at[number], merge_and_shift(kind_images, dx, dy))
        put_extended(charge_ext.at[number], merge_and_shift(charge_images, dx, dy))

    for number in range(AHEAD):
        spread_kind(number)
    charge_own = charge_images[(0, 0)] * Q_FACTOR
    for first, length, depths, base in RUNS:
        for sub in range(length):
            number = first + sub
            if number + AHEAD < len(SHIFTS):
                spread_kind(number + AHEAD)
            dx, dy = SHIFTS[number]
            chosen = half * 64 + category(x_site, dx) * 4 + category(y_site, dy)
            for turn, dz in enumerate(depths):
                place = base + sub * len(depths) + turn
                weight = lane_gather(weight_of[dz], chosen)
                rows = pl.ds(HALO + dz, ROWS)
                depth = depth_of(kind_ext[number, rows, :])
                coef_lj[place] = weight * depth
                coef_q[place] = weight * (charge_own * charge_ext[number, rows, :])

    def add_pair(scaled, force, place, number, dz):
        apart = [scaled[k] - ext[number, k, pl.ds(HALO + dz, ROWS), :] for k in range(3)]
        dist_sq = apart[0] * apart[0] + apart[1] * apart[1] + apart[2] * apart[2]
        inv_r = lax.rsqrt(dist_sq)
        inv_sq = inv_r * inv_r
        taper = jnp.maximum(REACH - dist_sq, 0.0)
        inv_4 = inv_sq * inv_sq
        inv_6 = inv_4 * inv_sq
        lennard = coef_lj[place] * (inv_4 * inv_4) * (inv_6 - 1.0)
        coulomb = coef_q[place] * (inv_sq * inv_r - Q_SHIFT)
        scalar = taper * taper * (lennard + coulomb)
        return [force[k] + scalar * apart[k] for k in range(3)]

    def advance(turn):
        mine = [now[component] for component in range(3)]
        images = []
        for component in range(3):
            found = gather_images(turn, component, mine[component])
            images.append({key: value * (1.0 / UNIT) for key, value in found.items()})
        scaled = [images[k][(0, 0)] for k in range(3)]
        force = [jnp.zeros((ROWS, LANES), jnp.float32) for _ in range(3)]
        for number in range(AHEAD):
            spread_position(images, number)
        for first, length, depths, base in RUNS:
            for sub in range(length):
                number = first + sub
                if number + AHEAD < len(SHIFTS):
                    spread_position(images, number + AHEAD)
                for which, dz in enumerate(depths):
                    force = add_pair(scaled, force, base + sub * len(depths) + which, number, dz)
        for k in range(3):
            new_speed = speed[k] + (TIME_STEP / MASS * UNIT) * force[k]
            speed[k] = new_speed
            now[k] = mine[k] + TIME_STEP * new_speed

    def turn_body(turn, carry):
        advance(turn)
        exchange(turn + 1, [now[component] for component in range(3)])
        for number in range(len(SIDES)):
            side_copy(turn + 1, number).wait_recv()
        return carry

    lax.fori_loop(0, STEPS - 1, turn_body, 0)
    advance(STEPS - 1)
    for component in range(3):
        out_pos_ref[component] = to_slots(now[component])
        out_vel_ref[component] = to_slots(speed[component])
    for turn in range(STEPS):
        for number in range(len(SIDES)):
            side_copy(turn, number).wait_send()
    for number in range(3):
        tile_copy(number).wait_send()


def per_device(n_gx, n_gy, positions, velocities, bead_types, eps_table, charges, x_list, y_list, tiles):
    beads = positions.shape[-1]
    strip = x_list.shape[-1]
    side = 2 * beads // strip
    shape = jax.ShapeDtypeStruct((3, ROWS, LANES), jnp.float32)
    vmem = pl.BlockSpec(memory_space=pltpu.VMEM)
    new_pos, new_vel = pl.pallas_call(
        functools.partial(kernel, n_gx, n_gy, side),
        out_shape=(shape, shape),
        in_specs=[vmem] * 6,
        out_specs=(vmem, vmem),
        scratch_shapes=[
            pltpu.VMEM((8, LANES), jnp.int32),
            pltpu.VMEM((3, 8, LANES), jnp.int32),
            pltpu.VMEM((STEPS, len(SIDES), ROWS, LANES), jnp.float32),
            pltpu.VMEM((STEPS, len(SIDES), ROWS, LANES), jnp.float32),
            pltpu.VMEM((len(SHIFTS), 3, ROWS + 2 * HALO, LANES), jnp.float32),
            pltpu.VMEM((len(SHIFTS), ROWS + 2 * HALO, LANES), jnp.int32),
            pltpu.VMEM((len(SHIFTS), ROWS + 2 * HALO, LANES), jnp.float32),
            pltpu.VMEM((COUNT, ROWS, LANES), jnp.float32),
            pltpu.VMEM((COUNT, ROWS, LANES), jnp.float32),
            pltpu.VMEM((3, ROWS, LANES), jnp.float32),
            pltpu.VMEM((3, ROWS, LANES), jnp.float32),
            pltpu.VMEM((ROWS, LANES), jnp.float32),
            pltpu.VMEM((ROWS, LANES), jnp.int32),
            pltpu.VMEM((LANES, LANES), jnp.float32),
            pltpu.VMEM((NTYPES, ROWS, LANES), jnp.float32),
            pltpu.SemaphoreType.DMA((2, 3)),
            pltpu.SemaphoreType.DMA((STEPS, len(SIDES))),
            pltpu.SemaphoreType.DMA((STEPS, len(SIDES))),
        ],
        compiler_params=pltpu.CompilerParams(collective_id=0, has_side_effects=True),
    )(
        positions.reshape(3, ROWS, LANES),
        velocities.reshape(3, ROWS, LANES),
        bead_types.reshape(ROWS, LANES),
        tiles.reshape(2, -1),
        eps_table,
        charges[None],
    )
    return new_pos.reshape(positions.shape), new_vel.reshape(velocities.shape)


def solution(mesh):
    return jax.shard_map(
        functools.partial(per_device, mesh.shape["gx"], mesh.shape["gy"]),
        mesh=mesh,
        in_specs=(
            P(None, "gx", "gy", None),
            P(None, "gx", "gy", None),
            P("gx", "gy", None),
            P(),
            P(),
            P("gx", "gy", None),
            P("gx", "gy", None),
            P("gx", "gy", None, None),
        ),
        out_specs=(P(None, "gx", "gy", None), P(None, "gx", "gy", None)),
        check_vma=False,
    )
```

profile of v0, /device:TPU:0, one launch (start us, length us, event | category | flops | bytes accessed | tf_op | source)
XLA Modules:
  0.0 44.4 jit_solution(16747759346903183550)
XLA Ops:
  0.6 41.8 %shard_map.77 = (f32[3,16,128]{2,1,0:T(8,128)}, f32[3,16,128]{2,1,0:T(8,128)}) custom-call(f32[3,16,128]{2,1,0:T(8,128)} %bitcast.7, f32[3,16,128]{2,1,0:T(8,128)} %bitcast.8, s32[16,128]{1,0:T(8,128)} %bitcast.11, s32[2,112]{1,0:T(2,128)} %bitcast.12, f32[18,18]{1,0:T(8,128)} %eps_ref.1, f32[1,18]{1,0:T(1,128)} %bitcast.13), custom_call_target="tpu_custom_call" | custom-call | tf_op jit(solution)/shard_map/pallas_call | solution.py:421
  42.4 0.0 copy-start
  42.4 1.4 %copy.14 = f32[3,1,1,2048]{3,2,1,0:T(1,128)} copy(f32[3,1,1,2048]{3,2,1,0:T(1,128)} %bitcast.10) | data formatting | bytes 49152
  43.8 0.0 copy-done
  43.8 0.6 %copy.15 = f32[3,1,1,2048]{3,2,1,0:T(1,128)} copy(f32[3,1,1,2048]{3,2,1,0:T(1,128)S(1)} %bitcast.9) | data formatting | bytes 49152
Async XLA Ops:
  42.4 1.4 %copy-start = (f32[3,16,128]{2,1,0:T(8,128)S(1)}, f32[3,16,128]{2,1,0:T(8,128)}, u32[]{:S(2)}) copy-start(f32[3,16,128]{2,1,0:T(8,128)} %get-tuple-element.5) | copy-start | bytes 73732
where the time goes:
time: 44.6 us; the launch traced here: 44.4 us
  Pallas kernels  41.8 us (94%)
  local copies, waits for them, and re-layouts  1.96 us (4%)
  between operations  0.65 us (1%)
    pallas_call x1, Pallas kernels, per_device(): pl.pallas_call(functools.partial(kernel, n_gx, n_gy, side), out_shape=(sh...  41.8 us
    unnamed x4, local copies, waits for them, and re-layouts  1.96 us

commit v1 on v0

--- a/solution.py
+++ b/solution.py
@@ -41,6 +41,18 @@
 Q_FACTOR = COULOMB / UNIT**3 * TAPER
 Q_SHIFT = (UNIT / CUTOFF) ** 3
 AHEAD = 3
+EDGES = [(-1, 0), (1, 0), (0, -1), (0, 1)]
+ORDER = [0, 2, 5, 7, 1, 6, 3, 4]
+FAR_STEPS = [0, 1, -1, 2, -2]
+HALO_TERMS = (
+    [(0, dz) for dz in (-2, -1, 0, 1, 2)]
+    + [(number, dz) for number in (1, 2) for dz in (-1, 0, 1)]
+    + [(3, 0), (4, 0)]
+    + [(5, dz) for dz in (-2, -1, 0, 1, 2)]
+    + [(6, dz) for dz in (-1, 0, 1)]
+    + [(7, dz) for dz in (-2, -1, 0)]
+)
+SPLIT = 3
 
 
 def lane_gather(values, index):
@@ -52,6 +64,7 @@
     pos_ref, vel_ref, kind_ref, tile_ref, eps_ref, charge_ref,
     out_pos_ref, out_vel_ref,
     tile_send, tile_recv, send, recv, ext, kind_ext, charge_ext, coef_lj, coef_q, now, speed, mix, site_ref, square, eps_own,
+    halo, halo_kind, halo_charge, halo_lj, halo_q, eps_edge, eps_near, edge, partial,
     tile_sems, send_sems, recv_sems,
 ):
     width = side * SPACING
@@ -139,17 +152,10 @@
         else:
             slot_of = lane >> 5
             inner = lane & 31
-            zh, yb, xb = inner >> 4, (inner >> 3) & 1, inner & 7
+            zh, yb, xb = inner >> 4, inner & 1, (inner >> 1) & 7
         x_low = side - 2 if sx > 0 else 0
         y_low = side - 2 if sy > 0 else 0
         return slot_of, zh * 64 + (yb + y_low) * 8 + xb + x_low
-
-    def unpack_index(sx, sy):
-        if sx != 0 and sy != 0:
-            return half * 4 + (y_site & 1) * 2 + (x_site & 1), 8
-        if sx != 0:
-            return half * 16 + y_site * 2 + (x_site & 1), 32
-        return half * 16 + (y_site & 1) * 8 + x_site, 32
 
     def pack(values, sx, sy):
         slot_of, source = pack_index(sx, sy)
@@ -180,28 +186,78 @@
             device_id_type=MESH,
         )
 
-    def image(turn, ux, uy, component):
-        number = SIDES.index((-ux, -uy))
-        index, stride = unpack_index(ux, uy)
-        return lane_gather(recv[turn, number], index + component * stride)
-
-    def merge_and_shift(images, dx, dy):
-        merged = images[(0, 0)]
-        in_x = (x_site < dx) if dx > 0 else (x_site >= side + dx)
-        in_y = (y_site < dy) if dy > 0 else (y_site >= side + dy)
-        ux = (dx > 0) - (dx < 0)
-        uy = (dy > 0) - (dy < 0)
-        if dx != 0:
-            merged = jnp.where(in_x, images[(ux, 0)], merged)
-        if dy != 0:
-            outer = images[(0, uy)]
-            if dx != 0:
-                outer = jnp.where(in_x, images[(ux, uy)], outer)
-            merged = jnp.where(in_y, outer, merged)
+    group = lane >> 6
+    far_side = (lane >> 5) & 1
+    z_half = (lane >> 4) & 1
+    along = (lane >> 1) & 7
+    bit = lane & 1
+    main = bit == far_side
+    across = far_side * (side - 2) + bit
+    x_edge = jnp.where(group == 0, across, along)
+    y_edge = jnp.where(group == 0, along, across)
+    edge_index = z_half * 64 + y_edge * 8 + x_edge
+    near_index = (lane & ~1) | far_side
+    turn_index = lane ^ 16
+    swap_index = lane ^ 1
+    block = lane & ~15
+    shift_by = jnp.where(far_side == 1, width, -width)
+    edge_shift = [jnp.where(group == 0, shift_by, 0.0), jnp.where(group == 1, shift_by, 0.0)]
+    corner_shift = [shift_by, jnp.where(along < 4, width, -width)]
+
+    def edges_of(turn, component):
+        merged = None
+        for k, (ux, uy) in enumerate(EDGES):
+            got = recv[turn, SIDES.index((-ux, -uy))]
+            if k != component:
+                got = pltpu.roll(got, ((k - component) * 32) % LANES, 1)
+            merged = got if merged is None else jnp.where((lane >> 5) == k, got, merged)
+        return merged
+
+    def corners_of(turn, component):
+        index = component * 8 + z_half * 4 + (along & 1) * 2 + bit
+        rows_of = []
+        for uy in (1, -1):
+            low = lane_gather(recv[turn, SIDES.index((1, -uy))], index)
+            high = lane_gather(recv[turn, SIDES.index((-1, -uy))], index)
+            rows_of.append(jnp.where(far_side == 0, low, high))
+        return jnp.where(along < 4, rows_of[0], rows_of[1])
+
+    def halo_step(number):
+        if number < 5:
+            return along * 0 + FAR_STEPS[number], bit
+        if number < 7:
+            return jnp.where(main, number - 4, 4 - number), 1 - far_side
+        return along * 0, 1 - far_side
+
+    def halo_shift(edges, corners, number):
+        if number == 0:
+            return edges
+        step, source_bit = halo_step(number)
+        place = along + step
+        index = block | ((place & 7) << 1) | source_bit
+        shifted = lane_gather(edges, index)
+        if number == 7:
+            return shifted
+        outside = ((place < 0) | (place > 7)) & (group == 0)
+        return jnp.where(outside, lane_gather(corners, index), shifted)
+
+    def put_halo(ref, values):
+        ref[pl.ds(HALO, ROWS), :] = values
+        turned = lane_gather(jnp.where(row8 < 4, values[:8], values[8:]), turn_index[:8])
+        ref[pl.ds(0, HALO), :] = turned
+        ref[pl.ds(HALO + ROWS, HALO), :] = turned
+
+    def halo_partner(ref, number, dz):
+        got = ref[pl.ds(HALO + dz, ROWS), :]
+        if number == 7 and dz + SPLIT <= 2:
+            got = jnp.where(main, got, ref[pl.ds(HALO + dz + SPLIT, ROWS), :])
+        return got
+
+    def own_shift(values, number):
+        dx, dy = SHIFTS[number]
         if dx == 0 and dy == 0:
-            return merged
-        source = half * 64 + ((y_site + dy) & 7) * 8 + ((x_site + dx) & 7)
-        return lane_gather(merged, source)
+            return values
+        return pltpu.roll(values, (-(8 * dy + dx)) % LANES, 1)
 
     def put_extended(ref, values):
         ref[pl.ds(HALO, ROWS), :] = values
@@ -209,27 +265,14 @@
         ref[pl.ds(0, HALO), :] = turned
         ref[pl.ds(HALO + ROWS, HALO), :] = turned
 
-    def gather_images(turn, component, own):
-        images = {(0, 0): own}
-        for ux, uy in SIDES:
-            got = image(turn, ux, uy, component)
-            if component == 0 and ux != 0:
-                got = got + ux * width
-            if component == 1 and uy != 0:
-                got = got + uy * width
-            images[(ux, uy)] = got
-        return images
-
     def exchange(turn, values):
-        for number, (sx, sy) in enumerate(SIDES):
-            send[turn, number] = pack(values, sx, sy)
-        for number in range(len(SIDES)):
+        for number in ORDER:
+            send[turn, number] = pack(values, *SIDES[number])
             side_copy(turn, number).start()
 
-    def spread_position(images, number):
-        dx, dy = SHIFTS[number]
+    def spread_position(scaled, number):
         for component in range(3):
-            put_extended(ext.at[number, component], merge_and_shift(images[component], dx, dy))
+            put_extended(ext.at[number, component], own_shift(scaled[component], number))
 
     square[...] = jnp.zeros((LANES, LANES), jnp.float32)
     square[0:NTYPES, 0:NTYPES] = eps_ref[...]
@@ -244,6 +287,59 @@
     exchange(0, own + [kind])
     for number in range(3):
         tile_copy(number).start()
+    kind_own = kind.astype(jnp.int32)
+    charge_plain = lane_gather(charge_row, kind_own)
+    for k in range(NTYPES):
+        row_k = jnp.broadcast_to(square[k : k + 1, :], (ROWS, LANES))
+        eps_own[k] = lane_gather(row_k, kind_own)
+
+    def depth_of(table, other):
+        level = [table[k] for k in range(NTYPES)] + [jnp.zeros((ROWS, LANES), jnp.float32)]
+        step = 1
+        while len(level) > 1:
+            odd = (other & step) != 0
+            joined = [jnp.where(odd, level[k + 1], level[k]) for k in range(0, len(level) - 1, 2)]
+            if len(level) % 2:
+                joined.append(level[-1])
+            level = joined
+            step = 2 * step
+        return level[0]
+
+    def spread_kind(number):
+        put_extended(kind_ext.at[number], own_shift(kind_own, number))
+        put_extended(charge_ext.at[number], own_shift(charge_plain, number))
+
+    for number in range(AHEAD):
+        spread_kind(number)
+    charge_own = charge_plain * Q_FACTOR
+    for first, length, depths, base in RUNS:
+        for sub in range(length):
+            number = first + sub
+            if number + AHEAD < len(SHIFTS):
+                spread_kind(number + AHEAD)
+            for turn, dz in enumerate(depths):
+                place = base + sub * len(depths) + turn
+                rows = pl.ds(HALO + dz, ROWS)
+                coef_lj[place] = depth_of(eps_own, kind_ext[number, rows, :])
+                coef_q[place] = charge_own * charge_ext[number, rows, :]
+
+    kind_edge = lane_gather(kind_own, edge_index)
+    kind_near = lane_gather(kind_edge, near_index)
+    for k in range(NTYPES):
+        row_k = jnp.broadcast_to(square[k : k + 1, :], (ROWS, LANES))
+        eps_edge[k] = lane_gather(row_k, kind_edge)
+        eps_near[k] = lane_gather(row_k, kind_near)
+    charge_edge = lane_gather(charge_row, kind_edge) * Q_FACTOR
+    charge_near = lane_gather(charge_row, kind_near) * Q_FACTOR
+
+    def put_edges(values):
+        for component in range(3):
+            scaled = lane_gather(values[component], edge_index) * (1.0 / UNIT)
+            edge[0, component] = scaled
+            edge[1, component] = lane_gather(scaled, near_index)
+
+    put_edges(own)
+
     for number in range(len(SIDES)):
         side_copy(0, number).wait_recv()
     for number in range(3):
@@ -315,93 +411,124 @@
             other >= side, 1, jnp.where(other < 0, 3, jnp.where((site < 2) & (other < 2), 2, 0))
         )
 
-    kind_images = gather_images(0, 3, kind)
-    kind_images = {key: value.astype(jnp.int32) for key, value in kind_images.items()}
-    charge_images = {key: lane_gather(charge_row, value) for key, value in kind_images.items()}
-    kind_own = kind_images[(0, 0)]
-    for k in range(NTYPES):
-        row_k = jnp.broadcast_to(square[k : k + 1, :], (ROWS, LANES))
-        eps_own[k] = lane_gather(row_k, kind_own)
-
-    def depth_of(other):
-        level = [eps_own[k] for k in range(NTYPES)] + [jnp.zeros((ROWS, LANES), jnp.float32)]
-        bit = 1
-        while len(level) > 1:
-            odd = (other & bit) != 0
-            joined = [jnp.where(odd, level[k + 1], level[k]) for k in range(0, len(level) - 1, 2)]
-            if len(level) % 2:
-                joined.append(level[-1])
-            level = joined
-            bit = 2 * bit
-        return level[0]
-
-    def spread_kind(number):
-        dx, dy = SHIFTS[number]
-        put_extended(kind_ext.at[number], merge_and_shift(kind_images, dx, dy))
-        put_extended(charge_ext.at[number], merge_and_shift(charge_images, dx, dy))
-
-    for number in range(AHEAD):
-        spread_kind(number)
-    charge_own = charge_images[(0, 0)] * Q_FACTOR
     for first, length, depths, base in RUNS:
         for sub in range(length):
-            number = first + sub
-            if number + AHEAD < len(SHIFTS):
-                spread_kind(number + AHEAD)
-            dx, dy = SHIFTS[number]
+            dx, dy = SHIFTS[first + sub]
             chosen = half * 64 + category(x_site, dx) * 4 + category(y_site, dy)
             for turn, dz in enumerate(depths):
                 place = base + sub * len(depths) + turn
                 weight = lane_gather(weight_of[dz], chosen)
-                rows = pl.ds(HALO + dz, ROWS)
-                depth = depth_of(kind_ext[number, rows, :])
-                coef_lj[place] = weight * depth
-                coef_q[place] = weight * (charge_own * charge_ext[number, rows, :])
-
-    def add_pair(scaled, force, place, number, dz):
-        apart = [scaled[k] - ext[number, k, pl.ds(HALO + dz, ROWS), :] for k in range(3)]
+                coef_lj[place] = weight * coef_lj[place]
+                coef_q[place] = weight * coef_q[place]
+
+    kind_edges = edges_of(0, 3).astype(jnp.int32)
+    kind_corners = corners_of(0, 3).astype(jnp.int32)
+    for number in range(8):
+        moved = halo_shift(kind_edges, kind_corners, number)
+        put_halo(halo_kind.at[number], moved)
+        put_halo(halo_charge.at[number], lane_gather(charge_row, moved))
+    for place, (number, dz) in enumerate(HALO_TERMS):
+        step, _ = halo_step(number)
+        inside = (group == 0) | ((along + step >= 0) & (along + step <= 7))
+        outward = 2 if number < 5 else 1
+        normal = jnp.where(far_side == 1, outward, -outward)
+        if number < 5:
+            start = across
+        else:
+            start = far_side * (side - 1)
+        place_x = jnp.where(group == 0, start, along)
+        place_y = jnp.where(group == 0, along, start)
+        step_x = jnp.where(group == 0, normal, step)
+        step_y = jnp.where(group == 0, step, normal)
+        chosen = z_half * 64 + category(place_x, step_x) * 4 + category(place_y, step_y)
+        weight = lane_gather(weight_of[dz], chosen)
+        if number == 7:
+            other = 0.0
+            if dz + SPLIT <= 2:
+                other = lane_gather(weight_of[dz + SPLIT], chosen)
+            weight = jnp.where(main, weight, other)
+        weight = jnp.where(inside, weight, 0.0)
+        table, charge_of = (eps_edge, charge_edge) if number < 5 else (eps_near, charge_near)
+        halo_lj[place] = weight * depth_of(table, halo_partner(halo_kind.at[number], number, dz))
+        halo_q[place] = weight * (charge_of * halo_partner(halo_charge.at[number], number, dz))
+
+    def pair_force(mine, partner, force, lj, charge):
+        apart = [mine[k] - partner[k] for k in range(3)]
         dist_sq = apart[0] * apart[0] + apart[1] * apart[1] + apart[2] * apart[2]
         inv_r = lax.rsqrt(dist_sq)
         inv_sq = inv_r * inv_r
         taper = jnp.maximum(REACH - dist_sq, 0.0)
         inv_4 = inv_sq * inv_sq
         inv_6 = inv_4 * inv_sq
-        lennard = coef_lj[place] * (inv_4 * inv_4) * (inv_6 - 1.0)
-        coulomb = coef_q[place] * (inv_sq * inv_r - Q_SHIFT)
+        lennard = lj * (inv_4 * inv_4) * (inv_6 - 1.0)
+        coulomb = charge * (inv_sq * inv_r - Q_SHIFT)
         scalar = taper * taper * (lennard + coulomb)
         return [force[k] + scalar * apart[k] for k in range(3)]
 
-    def advance(turn):
-        mine = [now[component] for component in range(3)]
-        images = []
-        for component in range(3):
-            found = gather_images(turn, component, mine[component])
-            images.append({key: value * (1.0 / UNIT) for key, value in found.items()})
-        scaled = [images[k][(0, 0)] for k in range(3)]
+    def own_forces():
+        scaled = [now[k] * (1.0 / UNIT) for k in range(3)]
         force = [jnp.zeros((ROWS, LANES), jnp.float32) for _ in range(3)]
         for number in range(AHEAD):
-            spread_position(images, number)
+            spread_position(scaled, number)
         for first, length, depths, base in RUNS:
             for sub in range(length):
                 number = first + sub
                 if number + AHEAD < len(SHIFTS):
-                    spread_position(images, number + AHEAD)
+                    spread_position(scaled, number + AHEAD)
                 for which, dz in enumerate(depths):
-                    force = add_pair(scaled, force, base + sub * len(depths) + which, number, dz)
+                    place = base + sub * len(depths) + which
+                    partner = [ext[number, k, pl.ds(HALO + dz, ROWS), :] for k in range(3)]
+                    force = pair_force(scaled, partner, force, coef_lj[place], coef_q[place])
         for k in range(3):
-            new_speed = speed[k] + (TIME_STEP / MASS * UNIT) * force[k]
+            partial[k] = force[k]
+
+    def finish(turn):
+        edges, corners = [], []
+        for component in range(3):
+            got = edges_of(turn, component)
+            far = corners_of(turn, component)
+            if component < 2:
+                got = got + edge_shift[component]
+                far = far + corner_shift[component]
+            edges.append(got * (1.0 / UNIT))
+            corners.append(far * (1.0 / UNIT))
+        for number in range(8):
+            for component in range(3):
+                put_halo(halo.at[number, component], halo_shift(edges[component], corners[component], number))
+        zero = [jnp.zeros((ROWS, LANES), jnp.float32) for _ in range(3)]
+        total = [zero, zero]
+        mine = [[edge[which, k] for k in range(3)] for which in range(2)]
+        for place, (number, dz) in enumerate(HALO_TERMS):
+            which = 0 if number < 5 else 1
+            partner = [halo_partner(halo.at[number, k], number, dz) for k in range(3)]
+            total[which] = pair_force(mine[which], partner, total[which], halo_lj[place], halo_q[place])
+        from_x = (x_site >> 2) * 32 + half * 16 + y_site * 2 + (x_site & 1)
+        from_y = 64 + (y_site >> 2) * 32 + half * 16 + x_site * 2 + (y_site & 1)
+        on_x = (x_site < 2) | (x_site >= side - 2)
+        on_y = (y_site < 2) | (y_site >= side - 2)
+        for k in range(3):
+            near = total[1][k] + lane_gather(total[1][k], swap_index)
+            merged = total[0][k] + jnp.where(main, near, 0.0)
+            force = partial[k]
+            force = force + jnp.where(on_x, lane_gather(merged, from_x), 0.0)
+            force = force + jnp.where(on_y, lane_gather(merged, from_y), 0.0)
+            new_speed = speed[k] + (TIME_STEP / MASS * UNIT) * force
             speed[k] = new_speed
-            now[k] = mine[k] + TIME_STEP * new_speed
+            now[k] = now[k] + TIME_STEP * new_speed
 
     def turn_body(turn, carry):
-        advance(turn)
-        exchange(turn + 1, [now[component] for component in range(3)])
+        finish(turn)
+        moved = [now[component] for component in range(3)]
+        exchange(turn + 1, moved)
+        put_edges(moved)
+        own_forces()
         for number in range(len(SIDES)):
             side_copy(turn + 1, number).wait_recv()
         return carry
 
+    own_forces()
     lax.fori_loop(0, STEPS - 1, turn_body, 0)
-    advance(STEPS - 1)
+    finish(STEPS - 1)
     for component in range(3):
         out_pos_ref[component] = to_slots(now[component])
         out_vel_ref[component] = to_slots(speed[component])
@@ -439,6 +566,15 @@
             pltpu.VMEM((ROWS, LANES), jnp.int32),
             pltpu.VMEM((LANES, LANES), jnp.float32),
             pltpu.VMEM((NTYPES, ROWS, LANES), jnp.float32),
+            pltpu.VMEM((8, 3, ROWS + 2 * HALO, LANES), jnp.float32),
+            pltpu.VMEM((8, ROWS + 2 * HALO, LANES), jnp.int32),
+            pltpu.VMEM((8, ROWS + 2 * HALO, LANES), jnp.float32),
+            pltpu.VMEM((len(HALO_TERMS), ROWS, LANES), jnp.float32),
+            pltpu.VMEM((len(HALO_TERMS), ROWS, LANES), jnp.float32),
+            pltpu.VMEM((NTYPES, ROWS, LANES), jnp.float32),
+            pltpu.VMEM((NTYPES, ROWS, LANES), jnp.float32),
+            pltpu.VMEM((2, 3, ROWS, LANES), jnp.float32),
+            pltpu.VMEM((3, ROWS, LANES), jnp.float32),
             pltpu.SemaphoreType.DMA((2, 3)),
             pltpu.SemaphoreType.DMA((STEPS, len(SIDES))),
             pltpu.SemaphoreType.DMA((STEPS, len(SIDES))),

time: 44.6 us -> 34.6 us (0.78)
  Pallas kernels: 41.8 us -> 31.8 us
    pallas_call x1, Pallas kernels: 41.8 us -> 31.8 us  [per_device(): pl.pallas_call(functools.partial(kernel, n_gx, n_gy, side), out_shape=(sh...]
where the time goes in v1:
time: 34.6 us; the launch traced here: 34.4 us
  Pallas kernels  31.8 us (92%)
  local copies, waits for them, and re-layouts  1.96 us (6%)
  between operations  0.65 us (2%)
    pallas_call x1, Pallas kernels, per_device(): pl.pallas_call(functools.partial(kernel, n_gx, n_gy, side), out_shape=(sh...  31.8 us
    unnamed x4, local copies, waits for them, and re-layouts  1.96 us

profile of v1, /device:TPU:0, one launch (start us, length us, event | category | flops | bytes accessed | tf_op | source)
XLA Modules:
  0.0 34.4 jit_solution(9415559386159361301)
XLA Ops:
  0.6 31.8 %shard_map.77 = (f32[3,16,128]{2,1,0:T(8,128)}, f32[3,16,128]{2,1,0:T(8,128)}) custom-call(f32[3,16,128]{2,1,0:T(8,128)} %bitcast.7, f32[3,16,128]{2,1,0:T(8,128)} %bitcast.8, s32[16,128]{1,0:T(8,128)} %bitcast.11, s32[2,112]{1,0:T(2,128)} %bitcast.12, f32[18,18]{1,0:T(8,128)} %eps_ref.1, f32[1,18]{1,0:T(1,128)} %bitcast.13), custom_call_target="tpu_custom_call" | custom-call | tf_op jit(solution)/shard_map/pallas_call | solution.py:548
  32.4 0.0 copy-start
  32.4 1.4 %copy.14 = f32[3,1,1,2048]{3,2,1,0:T(1,128)} copy(f32[3,1,1,2048]{3,2,1,0:T(1,128)} %bitcast.10) | data formatting | bytes 49152
  33.8 0.0 copy-done
  33.8 0.6 %copy.15 = f32[3,1,1,2048]{3,2,1,0:T(1,128)} copy(f32[3,1,1,2048]{3,2,1,0:T(1,128)S(1)} %bitcast.9) | data formatting | bytes 49152
Async XLA Ops:
  32.4 1.4 %copy-start = (f32[3,16,128]{2,1,0:T(8,128)S(1)}, f32[3,16,128]{2,1,0:T(8,128)}, u32[]{:S(2)}) copy-start(f32[3,16,128]{2,1,0:T(8,128)} %get-tuple-element.5) | copy-start | bytes 73732

commit v2 on v1

--- a/solution.py
+++ b/solution.py
@@ -62,8 +62,8 @@
 def kernel(
     n_gx, n_gy, side,
     pos_ref, vel_ref, kind_ref, tile_ref, eps_ref, charge_ref,
-    out_pos_ref, out_vel_ref,
-    tile_send, tile_recv, send, recv, ext, kind_ext, charge_ext, coef_lj, coef_q, now, speed, mix, site_ref, square, eps_own,
+    out_ref,
+    tile_send, tile_recv, send, recv, ext, kind_ext, charge_ext, coef_lj, coef_q, now, speed, mix, square, eps_own,
     halo, halo_kind, halo_charge, halo_lj, halo_q, eps_edge, eps_near, edge, partial,
     tile_sems, send_sems, recv_sems,
 ):
@@ -102,7 +102,6 @@
         + sx_f.astype(jnp.int32)
     )
     site = jnp.clip(site, 0, LANES - 1)
-    site_ref[...] = site
     big_row = lax.broadcasted_iota(jnp.int32, (LANES, LANES), 0)
     row8 = row[:8]
     parts = []
@@ -126,14 +125,6 @@
         mix[pl.ds(0, 8, stride=2), :] = even
         mix[pl.ds(1, 8, stride=2), :] = odd
         return mix[...]
-
-    def to_slots(values):
-        mix[...] = values
-        even = mix[pl.ds(0, 8, stride=2), :]
-        odd = mix[pl.ds(1, 8, stride=2), :]
-        first = jnp.where(low_half, even, pltpu.roll(odd, 64, 1))
-        second = jnp.where(low_half, pltpu.roll(even, 64, 1), odd)
-        return lane_gather(jnp.concatenate([first, second], axis=0), site_ref[...])
 
     for component in range(3):
         now[component] = to_lattice(pos_ref[component])
@@ -159,6 +150,14 @@
 
     def pack(values, sx, sy):
         slot_of, source = pack_index(sx, sy)
+        if sx != 0 and sy != 0:
+            packed = None
+            for part in range(2):
+                for component, value in enumerate(values):
+                    got = lane_gather(value[8 * part : 8 * part + 8], source[:8])
+                    take = (lane8 >> 3) == 4 * part + component
+                    packed = got if packed is None else jnp.where(take, got, packed)
+            return packed
         packed = lane_gather(values[0], source)
         for component in range(1, len(values)):
             packed = jnp.where(slot_of == component, lane_gather(values[component], source), packed)
@@ -166,9 +165,10 @@
 
     def side_copy(turn, number):
         sx, sy = SIDES[number]
+        rows = pl.ds(0, 8 if sx != 0 and sy != 0 else ROWS)
         return pltpu.make_async_remote_copy(
-            src_ref=send.at[turn, number],
-            dst_ref=recv.at[turn, number],
+            src_ref=send.at[turn, number, rows],
+            dst_ref=recv.at[turn, number, rows],
             send_sem=send_sems.at[turn, number],
             recv_sem=recv_sems.at[turn, number],
             device_id=at(sx, sy),
@@ -214,11 +214,16 @@
         return merged
 
     def corners_of(turn, component):
-        index = component * 8 + z_half * 4 + (along & 1) * 2 + bit
+        index = (component * 8 + z_half * 4 + (along & 1) * 2 + bit)[:8]
+
+        def one(number):
+            got = recv[turn, number, pl.ds(0, 8), :]
+            return jnp.concatenate([lane_gather(got, index), lane_gather(got, index + 32)], axis=0)
+
         rows_of = []
         for uy in (1, -1):
-            low = lane_gather(recv[turn, SIDES.index((1, -uy))], index)
-            high = lane_gather(recv[turn, SIDES.index((-1, -uy))], index)
+            low = one(SIDES.index((1, -uy)))
+            high = one(SIDES.index((-1, -uy)))
             rows_of.append(jnp.where(far_side == 0, low, high))
         return jnp.where(along < 4, rows_of[0], rows_of[1])
 
@@ -229,17 +234,26 @@
             return jnp.where(main, number - 4, 4 - number), 1 - far_side
         return along * 0, 1 - far_side
 
-    def halo_shift(edges, corners, number):
+    def halo_place(number):
+        step, source_bit = halo_step(number)
+        place = along + step
+        outside = ((place < 0) | (place > 7)) & (group == 0)
+        return block | ((place & 7) << 1) | source_bit, outside
+
+    def edge_part(edges, number):
         if number == 0:
             return edges
-        step, source_bit = halo_step(number)
-        place = along + step
-        index = block | ((place & 7) << 1) | source_bit
-        shifted = lane_gather(edges, index)
-        if number == 7:
+        return lane_gather(edges, halo_place(number)[0])
+
+    def corner_part(shifted, corners, number):
+        index, outside = halo_place(number)
+        return jnp.where(outside, lane_gather(corners, index), shifted)
+
+    def halo_shift(edges, corners, number):
+        shifted = edge_part(edges, number)
+        if number in (0, 7):
             return shifted
-        outside = ((place < 0) | (place > 7)) & (group == 0)
-        return jnp.where(outside, lane_gather(corners, index), shifted)
+        return corner_part(shifted, corners, number)
 
     def put_halo(ref, values):
         ref[pl.ds(HALO, ROWS), :] = values
@@ -267,7 +281,8 @@
 
     def exchange(turn, values):
         for number in ORDER:
-            send[turn, number] = pack(values, *SIDES[number])
+            packed = pack(values, *SIDES[number])
+            send[turn, number, pl.ds(0, packed.shape[0]), :] = packed
             side_copy(turn, number).start()
 
     def spread_position(scaled, number):
@@ -482,26 +497,41 @@
         for k in range(3):
             partial[k] = force[k]
 
-    def finish(turn):
-        edges, corners = [], []
-        for component in range(3):
-            got = edges_of(turn, component)
-            far = corners_of(turn, component)
-            if component < 2:
-                got = got + edge_shift[component]
-                far = far + corner_shift[component]
-            edges.append(got * (1.0 / UNIT))
-            corners.append(far * (1.0 / UNIT))
-        for number in range(8):
-            for component in range(3):
-                put_halo(halo.at[number, component], halo_shift(edges[component], corners[component], number))
-        zero = [jnp.zeros((ROWS, LANES), jnp.float32) for _ in range(3)]
-        total = [zero, zero]
+    zero = [jnp.zeros((ROWS, LANES), jnp.float32) for _ in range(3)]
+
+    def halo_forces(total, numbers):
         mine = [[edge[which, k] for k in range(3)] for which in range(2)]
+        total = list(total)
         for place, (number, dz) in enumerate(HALO_TERMS):
+            if number not in numbers:
+                continue
             which = 0 if number < 5 else 1
             partner = [halo_partner(halo.at[number, k], number, dz) for k in range(3)]
             total[which] = pair_force(mine[which], partner, total[which], halo_lj[place], halo_q[place])
+        return total
+
+    def begin(turn):
+        for component in range(3):
+            got = edges_of(turn, component)
+            if component < 2:
+                got = got + edge_shift[component]
+            got = got * (1.0 / UNIT)
+            for number in (0, 7):
+                put_halo(halo.at[number, component], edge_part(got, number))
+            for number in range(1, 7):
+                halo[number, component, pl.ds(HALO, ROWS), :] = edge_part(got, number)
+        return halo_forces([zero, zero], (0, 7))
+
+    def finish(turn, total):
+        for component in range(3):
+            far = corners_of(turn, component)
+            if component < 2:
+                far = far + corner_shift[component]
+            far = far * (1.0 / UNIT)
+            for number in range(1, 7):
+                shifted = halo[number, component, pl.ds(HALO, ROWS), :]
+                put_halo(halo.at[number, component], corner_part(shifted, far, number))
+        total = halo_forces(total, range(1, 7))
         from_x = (x_site >> 2) * 32 + half * 16 + y_site * 2 + (x_site & 1)
         from_y = 64 + (y_site >> 2) * 32 + half * 16 + x_site * 2 + (y_site & 1)
         on_x = (x_site < 2) | (x_site >= side - 2)
@@ -517,26 +547,52 @@
             now[k] = now[k] + TIME_STEP * new_speed
 
     def turn_body(turn, carry):
-        finish(turn)
-        moved = [now[component] for component in range(3)]
-        exchange(turn + 1, moved)
-        put_edges(moved)
         own_forces()
-        for number in range(len(SIDES)):
-            side_copy(turn + 1, number).wait_recv()
+
+        @pl.when(turn > 0)
+        def _():
+            for number in (3, 4, 1, 6):
+                side_copy(turn, number).wait_recv()
+
+        total = begin(turn)
+
+        @pl.when(turn > 0)
+        def _():
+            for number in (0, 2, 5, 7):
+                side_copy(turn, number).wait_recv()
+
+        finish(turn, total)
+
+        @pl.when(turn < STEPS - 1)
+        def _():
+            moved = [now[component] for component in range(3)]
+            exchange(turn + 1, moved)
+            put_edges(moved)
+
         return carry
 
-    own_forces()
-    lax.fori_loop(0, STEPS - 1, turn_body, 0)
-    finish(STEPS - 1)
+    lax.fori_loop(0, STEPS, turn_body, 0)
     for component in range(3):
-        out_pos_ref[component] = to_slots(now[component])
-        out_vel_ref[component] = to_slots(speed[component])
+        out_ref[component] = now[component]
+        out_ref[3 + component] = speed[component]
+    out_ref[6] = site.astype(jnp.float32)
     for turn in range(STEPS):
         for number in range(len(SIDES)):
             side_copy(turn, number).wait_send()
     for number in range(3):
         tile_copy(number).wait_send()
+
+
+def reorder(in_ref, out_pos_ref, out_vel_ref):
+    low_half = lax.broadcasted_iota(jnp.int32, (8, LANES), 1) < 64
+    site = in_ref[6].astype(jnp.int32)
+    for which in range(6):
+        even = in_ref[which, pl.ds(0, 8, stride=2), :]
+        odd = in_ref[which, pl.ds(1, 8, stride=2), :]
+        first = jnp.where(low_half, even, pltpu.roll(odd, 64, 1))
+        second = jnp.where(low_half, pltpu.roll(even, 64, 1), odd)
+        out = out_pos_ref if which < 3 else out_vel_ref
+        out[which % 3] = lane_gather(jnp.concatenate([first, second], axis=0), site)
 
 
 def per_device(n_gx, n_gy, positions, velocities, bead_types, eps_table, charges, x_list, y_list, tiles):
@@ -545,11 +601,11 @@
     side = 2 * beads // strip
     shape = jax.ShapeDtypeStruct((3, ROWS, LANES), jnp.float32)
     vmem = pl.BlockSpec(memory_space=pltpu.VMEM)
-    new_pos, new_vel = pl.pallas_call(
+    moved = pl.pallas_call(
         functools.partial(kernel, n_gx, n_gy, side),
-        out_shape=(shape, shape),
+        out_shape=jax.ShapeDtypeStruct((7, ROWS, LANES), jnp.float32),
         in_specs=[vmem] * 6,
-        out_specs=(vmem, vmem),
+        out_specs=vmem,
         scratch_shapes=[
             pltpu.VMEM((8, LANES), jnp.int32),
             pltpu.VMEM((3, 8, LANES), jnp.int32),
@@ -563,7 +619,6 @@
             pltpu.VMEM((3, ROWS, LANES), jnp.float32),
             pltpu.VMEM((3, ROWS, LANES), jnp.float32),
             pltpu.VMEM((ROWS, LANES), jnp.float32),
-            pltpu.VMEM((ROWS, LANES), jnp.int32),
             pltpu.VMEM((LANES, LANES), jnp.float32),
             pltpu.VMEM((NTYPES, ROWS, LANES), jnp.float32),
             pltpu.VMEM((8, 3, ROWS + 2 * HALO, LANES), jnp.float32),
@@ -588,6 +643,12 @@
         eps_table,
         charges[None],
     )
+    new_pos, new_vel = pl.pallas_call(
+        reorder,
+        out_shape=(shape, shape),
+        in_specs=[vmem],
+        out_specs=(vmem, vmem),
+    )(moved)
     return new_pos.reshape(positions.shape), new_vel.reshape(velocities.shape)
 
 

time: 34.6 us -> 32 us (0.925)
  local copies, waits for them, and re-layouts: 1.96 us -> 0 us
  Pallas kernels: 31.8 us -> 31.1 us
    unnamed x4 -> x0, local copies, waits for them, and re-layouts: 1.96 us -> none
    pallas_call x1 -> x2, Pallas kernels: 31.8 us -> 31.1 us  [the longest x1 29.5 us: per_device(): pl.pallas_call(functools.partial(kernel, n_gx, n_gy, side), out_shape=jax...]
where the time goes in v2:
time: 32 us; the launch traced here: 31.8 us
  Pallas kernels  31.1 us (97%)
  between operations  0.64 us (2%)
    pallas_call x1, Pallas kernels, per_device(): pl.pallas_call(functools.partial(kernel, n_gx, n_gy, side), out_shape=jax...  29.5 us
    pallas_call x1, Pallas kernels, per_device(): pl.pallas_call(reorder, out_shape=(shape, shape), in_specs=[vmem], out_sp...  1.59 us

profile of v2, /device:TPU:0, one launch (start us, length us, event | category | flops | bytes accessed | tf_op | source)
XLA Modules:
  0.0 31.8 jit_solution(3257299032589118075)
XLA Ops:
  0.6 29.5 %shard_map.77.in_ref = f32[7,16,128]{2,1,0:T(8,128)} custom-call(f32[3,16,128]{2,1,0:T(8,128)} %bitcast.7, f32[3,16,128]{2,1,0:T(8,128)} %bitcast.8, s32[16,128]{1,0:T(8,128)} %bitcast.9, s32[2,112]{1,0:T(2,128)} %bitcast.10, f32[18,18]{1,0:T(8,128)} %eps_ref.1, f32[1,18]{1,0:T(1,128)} %bitcast.11), custom_call_target="tpu_custom_call" | custom-call | tf_op jit(solution)/shard_map/pallas_call | solution.py:604
  30.2 1.6 %shard_map.78 = (f32[3,16,128]{2,1,0:T(8,128)}, f32[3,16,128]{2,1,0:T(8,128)}) custom-call(f32[7,16,128]{2,1,0:T(8,128)} %shard_map.77.in_ref), custom_call_target="tpu_custom_call" | custom-call | tf_op jit(solution)/shard_map/pallas_call | solution.py:646
